TPU v7x, 128 devices: a whole 4x4x4 slice. The times are simulated.
128 devices in a mesh: ctx: 8 (over x, z_lo), head: 16 (over z_hi, y, core).
Axes of the slice: x: 4, y: 4, z: 4 (z_hi: 2, z_lo: 2; z = z_hi * 2 + z_lo), core: 2. Of those that a mesh axis runs over, the one named last changes fastest.
Arguments:
- queries: bfloat16 [256, 16384], P(None, 'head'), may hold values from -64 to 64, as said below
- grad_out: bfloat16 [256, 16384], P(None, 'head'), may hold values from -24 to 24
- latent: bfloat16 [16384, 512], P(('ctx', 'head')), may hold values from -6.1 to 6.1
- up_key: bfloat16 [512, 16384], P(None, 'head'), as said below
- up_value: bfloat16 [512, 16384], P(None, 'head'), may hold values from -0.25 to 0.25
Outputs:
- grad_queries: float32 [256, 16384], P('ctx', 'head')
- grad_latent: float32 [16384, 512], P(('ctx', 'head'))
- grad_up_key: float32 [512, 16384], P('ctx', 'head')
- grad_up_value: float32 [512, 16384], P('ctx', 'head')
Inputs may be any that keep to these rules, and one draw needn't show every extreme that they name: `queries`: entries lie within 64 in magnitude. `up_key`: entries lie within 4 / sqrt(512) in magnitude.
All inputs are finite; a program needn't handle non-finite values.
Results may differ from a plain program's by a relative error of at most 0.005.
Values may be sent and summed in bfloat16 or wider, within the bound.
A program may use at most 128 MiB of HBM per device.

v0:
```python
import math
import jax
import jax.numpy as jnp
from jax import lax
from jax.sharding import PartitionSpec as P

HD = 128


def joined(part, axis, combine):
    gathered = jax.tree.map(lambda a: lax.all_gather(a, axis), part)

    def take(source):
        return jax.tree.map(lambda a: lax.dynamic_index_in_dim(a, source, 0, False), gathered)

    return lax.fori_loop(
        1, lax.axis_size(axis), lambda source, state: combine(state, take(source)), take(0)
    )


def join_pairs(former, latter):
    maxima = jnp.maximum(former[0], latter[0])
    left_factor = jnp.exp(former[0] - maxima)
    right_factor = jnp.exp(latter[0] - maxima)
    return (maxima, former[1] * left_factor + latter[1] * right_factor)


def local(queries, grad_out, latent, up_key, up_value):
    scale = 1.0 / math.sqrt(HD)
    local_heads = queries.shape[1] // HD
    width = queries.shape[1]
    query_count = queries.shape[0]
    contract_cols = (((1,), (1,)), ((), ()))
    contract_rows = (((0,), (0,)), ((), ()))
    block = lax.all_gather(latent, "head", axis=0, tiled=True)
    key_rows = block.shape[0]
    total_len = key_rows * lax.axis_size("ctx")
    first_key = lax.axis_index("ctx") * key_rows
    key_block = jnp.dot(block, up_key, preferred_element_type=jnp.float32)
    value_block = jnp.dot(block, up_value, preferred_element_type=jnp.float32).astype(jnp.bfloat16)
    query_pos = total_len - query_count + lax.iota(jnp.int32, query_count)
    key_pos = first_key + lax.iota(jnp.int32, key_rows)
    visible = key_pos[None, :] <= query_pos[:, None]
    head_ids = jnp.arange(local_heads, dtype=jnp.int32)

    def head_inputs(head_index):
        offset = head_index * HD
        return (
            lax.dynamic_slice_in_dim(queries, offset, HD, 1),
            lax.dynamic_slice_in_dim(grad_out, offset, HD, 1),
            lax.dynamic_slice_in_dim(key_block, offset, HD, 1),
            lax.dynamic_slice_in_dim(value_block, offset, HD, 1),
        )

    def masked_scores(query_head, key_head):
        raw = (
            lax.dot_general(
                query_head.astype(jnp.float32),
                key_head,
                contract_cols,
                precision=lax.Precision.HIGHEST,
            )
            * scale
        )
        return jnp.where(visible, raw, -jnp.inf)

    def product_scores(grad_head, value_head):
        return lax.dot_general(
            grad_head, value_head, contract_cols, preferred_element_type=jnp.float32
        )

    def pick_row(table, head_index):
        return lax.dynamic_index_in_dim(table, head_index, 0, keepdims=False)

    def local_pair(head_index):
        query_head, grad_head, key_head, value_head = head_inputs(head_index)
        scores = masked_scores(query_head, key_head)
        maxima = jnp.max(scores, axis=1)
        return (maxima, jnp.sum(jnp.exp(scores - maxima[:, None]), axis=1))

    local_max, local_sum = lax.map(local_pair, head_ids)
    maxima, totals = joined((local_max, local_sum), "ctx", join_pairs)

    def local_delta(head_index):
        query_head, grad_head, key_head, value_head = head_inputs(head_index)
        scores = masked_scores(query_head, key_head)
        probs = (
            jnp.exp(scores - pick_row(maxima, head_index)[:, None])
            / pick_row(totals, head_index)[:, None]
        )
        return jnp.sum(probs * product_scores(grad_head, value_head), axis=1)

    deltas = lax.psum(lax.map(local_delta, head_ids), "ctx")

    def accumulate(head_index, carry):
        query_acc, grad_kv = carry
        query_head, grad_head, key_head, value_head = head_inputs(head_index)
        scores = masked_scores(query_head, key_head)
        probs = (
            jnp.exp(scores - pick_row(maxima, head_index)[:, None])
            / pick_row(totals, head_index)[:, None]
        )
        grad_probs = product_scores(grad_head, value_head)
        grad_scores = (probs * (grad_probs - pick_row(deltas, head_index)[:, None]) * scale).astype(
            jnp.bfloat16
        )
        query_part = jnp.dot(
            grad_scores.astype(jnp.float32), key_head, precision=lax.Precision.HIGHEST
        )
        key_grad = lax.dot_general(
            grad_scores, query_head, contract_rows, preferred_element_type=jnp.float32
        ).astype(jnp.bfloat16)
        value_grad = lax.dot_general(
            probs.astype(jnp.bfloat16), grad_head, contract_rows, preferred_element_type=jnp.float32
        ).astype(jnp.bfloat16)
        offset = head_index * HD
        anchor = jnp.zeros((), jnp.int32)
        query_acc = lax.dynamic_update_slice(query_acc, query_part, (anchor, offset))
        grad_kv = lax.dynamic_update_slice(grad_kv, key_grad, (anchor, offset))
        grad_kv = lax.dynamic_update_slice(grad_kv, value_grad, (anchor, width + offset))
        return (query_acc, grad_kv)

    start_state = (
        jnp.zeros((query_count, width), jnp.float32),
        jnp.zeros((key_rows, 2 * width), jnp.bfloat16),
    )
    query_acc, grad_kv = lax.fori_loop(0, local_heads, accumulate, start_state)
    up_both = jnp.concatenate([up_key, up_value], axis=1)
    grad_queries = lax.psum_scatter(query_acc, "ctx", scatter_dimension=0, tiled=True)
    weight_sums = lax.psum_scatter(
        lax.dot_general(block, grad_kv, contract_rows, preferred_element_type=jnp.float32),
        "ctx",
        scatter_dimension=0,
        tiled=True,
    )
    own_rows = latent.shape[0]
    summed = lax.psum(
        lax.dot_general(grad_kv, up_both, contract_cols, preferred_element_type=jnp.float32), "head"
    )
    grad_latent = lax.dynamic_slice_in_dim(summed, lax.axis_index("head") * own_rows, own_rows, 0)
    return (grad_queries, grad_latent, weight_sums[:, :width], weight_sums[:, width:])


def solution(mesh):
    return jax.shard_map(
        local,
        mesh=mesh,
        in_specs=(
            P(None, "head"),
            P(None, "head"),
            P(("ctx", "head"), None),
            P(None, "head"),
            P(None, "head"),
        ),
        out_specs=(P("ctx", "head"), P(("ctx", "head"), None), P("ctx", "head"), P("ctx", "head")),
        check_vma=False,
    )
```

profile of v0, /device:TPU:0, one launch (start us, length us, event | category | flops | bytes accessed | tf_op | source)
XLA Modules:
  0.0 633.1 jit_solution(3696228629027708976)
XLA Ops:
  8.0 53.2 %all-gather.4.cloned.1.call-done = bf16[2048,512]{1,0:T(8,128)(2,1)} async-done(((bf16[128,512]{1,0:T(8,128)(2,1)}), bf16[2048,512]{1,0:T(8,128)(2,1)}) %all-gather.4.cloned.1.call-update) | async-done | bytes 2097168 | tf_op jit(solution)/shard_map/all_gather | solution.py:35
  61.2 7.4 %fusion.52 = f32[2048,1024]{1,0:T(8,128)} fusion(bf16[2048,512]{1,0:T(8,128)(2,1)} %all-gather.4.cloned.1.call-done, bf16[512,1024]{1,0:T(8,128)(2,1)} %param.16), kind=kOutput, calls=%fused_computation.71 | convolution fusion | flops 2147483648 | bytes 11534336 | tf_op jit(solution)/shard_map/dot_general | solution.py:39
  68.6 34.9 %while.60 = (s32[]{:T(128)}, f32[8,256]{1,0:T(8,128)S(1)}, f32[8,256]{1,0:T(8,128)S(1)}, s32[8]{0:T(128)S(1)}, bf16[256,1024]{1,0:T(8,128)(2,1)S(1)}, /*index=5*...) while((s32[]{:T(128)}, f32[8,256]{1,0:T(8,128)S(1)}, ...), condition=%wide.region_3.4_spmd.clone, body=%wide.region_0.3_spmd.clone.sunk | while | flops 808451584 | bytes 5326015 | solution.py:81
  69.9 2.5 fusion.85
  74.3 2.5 fusion.85
  78.7 2.5 fusion.85
  83.0 2.5 fusion.85
  87.4 2.5 fusion.85
  91.7 2.5 fusion.85
  96.1 2.5 fusion.85
  100.5 2.5 fusion.85
  103.6 28.2 %all-gather.1 = f32[64,256]{1,0:T(8,128)S(1)} all-gather(f32[8,256]{1,0:T(8,128)S(1)} %get-tuple-element.493), channel_id=3, replica_groups=mesh['ctx'=8,'head'=16] {'ctx'}, dimensions={0}, use_global_device_ids=true | all-gather | bytes 73728 | tf_op jit(solution)/shard_map/all_gather | solution.py:11
  131.8 28.2 %all-gather = f32[64,256]{1,0:T(8,128)S(1)} all-gather(f32[8,256]{1,0:T(8,128)S(1)} %get-tuple-element.492), channel_id=2, replica_groups=mesh['ctx'=8,'head'=16] {'ctx'}, dimensions={0}, use_global_device_ids=true | all-gather | bytes 73728 | tf_op jit(solution)/shard_map/all_gather | solution.py:11
  160.2 5.9 convolution_convert_fusion.2
  166.1 60.3 %while.61 = (s32[]{:T(128)}, f32[8,256]{1,0:T(8,128)S(1)}, s32[8]{0:T(128)S(1)}, bf16[256,1024]{1,0:T(8,128)(2,1)S(1)}, f32[2048,1024]{1,0:T(8,128)}, /*index=5*...) while((s32[]{:T(128)}, f32[8,256]{1,0:T(8,128)S(1)}, ...), condition=%wide.region_8.9_spmd.clone, body=%wide.region_6.8_spmd.clone.sunk | while | flops 943193856 | bytes 5918977 | solution.py:93
  169.3 2.7 fusion.90
  176.9 2.7 fusion.90
  184.4 2.7 fusion.90
  191.9 2.7 fusion.90
  199.5 2.7 fusion.90
  207.0 2.7 fusion.90
  214.6 2.7 fusion.90
  222.1 2.7 fusion.90
  226.5 19.1 %psum.14 = f32[8,256]{1,0:T(8,128)S(1)} all-reduce(f32[8,256]{1,0:T(8,128)S(1)} %get-tuple-element.496), channel_id=1, replica_groups=mesh['ctx'=8,'head'=16] {'ctx'}, use_global_device_ids=true, to_apply=%region_9.10 | all-reduce | flops 2048 | bytes 16384 | tf_op jit(solution)/shard_map/psum | solution.py:93
  245.7 4.3 broadcast_in_dim.48
  250.0 80.9 %while.62 = (s32[]{:T(128)}, f32[256,1024]{1,0:T(8,128)S(1)}, bf16[2048,2048]{1,0:T(8,128)(2,1)}, bf16[256,1024]{1,0:T(8,128)(2,1)S(1)}, f32[2048,1024]{1,0:T(8,...) while((s32[]{:T(128)}, f32[256,1024]{1,0:T(8,128)S(1)}, ...), condition=%wide.region_11.12_spmd.clone, body=%wide.region_10.11_spmd.clone.sunk | while | flops 2019033088 | bytes 13522222 | solution.py:127
  250.0 2.8 fusion.102
  254.3 2.3 convolution_dynamic-update-slice_fusion.2
  260.2 2.7 fusion.102
  264.4 2.3 convolution_dynamic-update-slice_fusion.2
  270.3 2.7 fusion.102
  274.5 2.3 convolution_dynamic-update-slice_fusion.2
  280.4 2.7 fusion.102
  284.7 2.3 convolution_dynamic-update-slice_fusion.2
  290.5 2.7 fusion.102
  294.7 2.3 convolution_dynamic-update-slice_fusion.2
  300.6 2.7 fusion.102
  304.9 2.3 convolution_dynamic-update-slice_fusion.2
  310.7 2.7 fusion.102
  314.9 2.3 convolution_dynamic-update-slice_fusion.2
  320.8 2.7 fusion.102
  325.0 2.3 convolution_dynamic-update-slice_fusion.2
  330.9 10.5 %fusion.45 = f32[2048,512]{1,0:T(8,128)} fusion(bf16[2048,2048]{1,0:T(8,128)(2,1)} %get-tuple-element.498, bf16[512,1024]{1,0:T(8,128)(2,1)} %param.17, bf16[512,1024]{1,0:T(8,128)(2,1)S(1)} %copy-done.3), kind=kOutput, calls=%fused_computation.61 | convolution fusion | flops 4299161600 | bytes 14680064 | tf_op jit(solution)/shard_map/dot_general | solution.py:138
  343.0 9.8 %convolution_bitcast_fusion = f32[512,2048]{0,1:T(8,128)} fusion(bf16[2048,2048]{1,0:T(8,128)(2,1)} %get-tuple-element.498, bf16[2048,512]{1,0:T(8,128)(2,1)S(1)} %copy-done.2), kind=kOutput, calls=%fused_computation.60 | convolution fusion | flops 4294967296 | bytes 14680064 | tf_op jit(solution)/shard_map/dot_general | solution.py:131
  352.8 5.5 copy.13
  358.8 130.5 %all-reduce.2.cloned.1.call-done = f32[2048,512]{1,0:T(8,128)} async-done(((f32[2048,512]{1,0:T(8,128)}), f32[2048,512]{1,0:T(8,128)}) %all-reduce.2.cloned.1.call-update) | async-done | bytes 4194320 | tf_op jit(solution)/shard_map/psum | solution.py:137
  491.1 91.7 %reduce-scatter.7.cloned.1.call-done = f32[64,2048]{1,0:T(8,128)} async-done(((f32[512,2048]{1,0:T(8,128)}), f32[64,2048]{1,0:T(8,128)}) %reduce-scatter.7.cloned.1.call-update) | async-done | bytes 524304
  584.6 41.9 %reduce-scatter.5.cloned.1.call-done = f32[32,1024]{1,0:T(8,128)} async-done(((f32[256,1024]{1,0:T(8,128)}), f32[32,1024]{1,0:T(8,128)}) %reduce-scatter.5.cloned.1.call-update) | async-done | bytes 131088 | tf_op jit(solution)/shard_map/reduce_scatter | solution.py:129
  (142 shorter events, 75.2 us)
Async XLA Ops:
  7.2 54.0 %all-gather.4.cloned.1.call-start = ((), (), s32[]{:S(2)}) async-start(), calls=%async_computation.2 | async-start | bytes 2228224 | tf_op jit(solution)/shard_map/all_gather | solution.py:35
  7.9 481.5 %all-reduce.2.cloned.1.call-start = ((), (), s32[]{:S(2)}) async-start(), calls=%async_computation.4 | async-start | bytes 8388608 | tf_op jit(solution)/shard_map/psum | solution.py:137
  8.0 60.7 %copy-start.1 = (bf16[256,1024]{1,0:T(8,128)(2,1)S(1)}, bf16[256,1024]{1,0:T(8,128)(2,1)}, u32[]{:S(2)}) copy-start(bf16[256,1024]{1,0:T(8,128)(2,1)} %param.13) | copy-start | bytes 1572868
  68.6 91.6 %copy-start.4 = (bf16[512,1024]{1,0:T(8,128)(2,1)S(1)}, bf16[512,1024]{1,0:T(8,128)(2,1)}, u32[]{:S(2)}) copy-start(bf16[512,1024]{1,0:T(8,128)(2,1)} %param.17) | copy-start | bytes 3145732
  250.0 80.9 %copy-start.3 = (bf16[512,1024]{1,0:T(8,128)(2,1)S(1)}, bf16[512,1024]{1,0:T(8,128)(2,1)}, u32[]{:S(2)}) copy-start(bf16[512,1024]{1,0:T(8,128)(2,1)} %param.16) | copy-start | bytes 3145732
  330.9 10.5 %copy-start = (f32[256,1024]{1,0:T(8,128)}, f32[256,1024]{1,0:T(8,128)S(1)}, u32[]{:S(2)}) copy-start(f32[256,1024]{1,0:T(8,128)S(1)} %get-tuple-element.497) | copy-start | bytes 3145732
  341.4 1.6 copy-start.2
  341.4 241.3 %reduce-scatter.7.cloned.1.call-start = ((), (), s32[]{:S(2)}) async-start(), calls=%async_computation.5 | async-start | bytes 4718592
  358.3 268.3 %reduce-scatter.5.cloned.1.call-start = ((), (), s32[]{:S(2)}) async-start(), calls=%async_computation.3 | async-start | bytes 1179648 | tf_op jit(solution)/shard_map/reduce_scatter | solution.py:129
Sparse Core Ops, SparseCore 0:
  10.4 50.7 all-gather.3
  341.6 147.7 all-reduce.1
  491.8 90.8 reduce-scatter.6
  585.5 40.9 reduce-scatter.4
where the time goes:
time: 636 us; the launch traced here: 633 us
  waiting for transfers between devices  319 us (50%)
  matrix products  169 us (27%)
  blocking collectives  75.5 us (12%)
  loops' own time  26.6 us (4%)
  local copies, waits for them, and re-layouts  25.9 us (4%)
  between operations  13.9 us (2%)
    psum x1, waiting for transfers between devices, local(): lax.psum(lax.dot_general(grad_kv, up_both, contract_cols, preferred_eleme...  131 us
    unnamed x5, waiting for transfers between devices  92.9 us
    dot_general x24, matrix products, masked_scores(): lax.dot_general(query_head.astype(jnp.float32), key_head, contract_cols,...  63.4 us
    all_gather x2, blocking collectives, joined(): gathered = jax.tree.map(lambda a: lax.all_gather(a, axis), part)  56.4 us
    all_gather x1, waiting for transfers between devices, local(): block = lax.all_gather(latent, 'head', axis=0, tiled=True)  53.2 us
    reduce_scatter x1, waiting for transfers between devices, local(): lax.psum_scatter(query_acc, 'ctx', scatter_dimension=0, tiled=True)  41.9 us
    dot_general x16, matrix products, product_scores(): lax.dot_general(grad_head, value_head, contract_cols, preferred_element_t...  25.1 us
    another operation x1, loops' own time, local(): deltas = lax.psum(lax.map(local_delta, head_ids), 'ctx')  21 us
  transfers between devices with their start and end apart: 4, of which 4 were waited for; matrix products, arithmetic and copies ran while one was open for 3% of the time, Pallas kernels for 0%

commit v1 on v0

--- a/solution.py
+++ b/solution.py
@@ -32,7 +32,9 @@
     query_count = queries.shape[0]
     contract_cols = (((1,), (1,)), ((), ()))
     contract_rows = (((0,), (0,)), ((), ()))
-    block = lax.all_gather(latent, "head", axis=0, tiled=True)
+    block = jnp.concatenate(
+        lax.all_to_all(jnp.stack([latent] * lax.axis_size("head")), "head", 0, 0), axis=0
+    )
     key_rows = block.shape[0]
     total_len = key_rows * lax.axis_size("ctx")
     first_key = lax.axis_index("ctx") * key_rows

time: 636 us -> 520 us (0.82)
  waiting for transfers between devices: 319 us -> 187 us
  starting transfers between devices: 0.16 us -> 8.26 us
    unnamed x5 -> x4, waiting for transfers between devices: 92.9 us -> 0.57 us
    all_gather x1 -> x0, waiting for transfers between devices: 53.2 us -> none  [local(): block = lax.all_gather(latent, 'head', axis=0, tiled=True)]
    all_to_all x0 -> x1, waiting for transfers between devices: none -> 29.1 us  [local(): lax.all_to_all(jnp.stack([latent] * lax.axis_size('head')), 'head', 0, 0)]
    reduce_scatter x1, waiting for transfers between devices: 41.9 us -> 15.6 us  [local(): lax.psum_scatter(query_acc, 'ctx', scatter_dimension=0, tiled=True)]
    psum x1, waiting for transfers between devices: 131 us -> 142 us  [local(): lax.psum(lax.dot_general(grad_kv, up_both, contract_cols, preferred_eleme...]
    all_to_all x0 -> x1, starting transfers between devices: none -> 8.13 us  [local(): lax.all_to_all(jnp.stack([latent] * lax.axis_size('head')), 'head', 0, 0)]
    dot_general x8, matrix products: 11 us -> 17.7 us  [accumulate(): lax.dot_general(grad_scores, query_head, contract_rows, preferred_element...]
  transfers between devices with their start and end apart: 4 -> 4, of which waited for: 4 -> 3; matrix products, arithmetic and copies ran while one was open for 3% -> 4% of each run, Pallas kernels for 0% -> 0%
where the time goes in v1:
time: 520 us; the launch traced here: 517 us
  waiting for transfers between devices  187 us (36%)
  matrix products  173 us (33%)
  blocking collectives  76 us (15%)
  loops' own time  26.6 us (5%)
  local copies, waits for them, and re-layouts  26.4 us (5%)
  between operations  15.6 us (3%)
  starting transfers between devices  8.26 us (2%)
    psum x1, waiting for transfers between devices, local(): lax.psum(lax.dot_general(grad_kv, up_both, contract_cols, preferred_eleme...  142 us
    dot_general x24, matrix products, masked_scores(): lax.dot_general(query_head.astype(jnp.float32), key_head, contract_cols,...  64.2 us
    all_gather x2, blocking collectives, joined(): gathered = jax.tree.map(lambda a: lax.all_gather(a, axis), part)  56.4 us
    all_to_all x1, waiting for transfers between devices, local(): lax.all_to_all(jnp.stack([latent] * lax.axis_size('head')), 'head', 0, 0)  29.1 us
    dot_general x16, matrix products, product_scores(): lax.dot_general(grad_head, value_head, contract_cols, preferred_element_t...  25.1 us
    another operation x1, loops' own time, local(): deltas = lax.psum(lax.map(local_delta, head_ids), 'ctx')  21 us
    psum x1, blocking collectives, local(): deltas = lax.psum(lax.map(local_delta, head_ids), 'ctx')  19.5 us
    dot_general x8, matrix products, accumulate(): jnp.dot(grad_scores.astype(jnp.float32), key_head, precision=lax.Precisio...  18.1 us
  transfers between devices with their start and end apart: 4, of which 3 were waited for; matrix products, arithmetic and copies ran while one was open for 4% of the time, Pallas kernels for 0%

profile of v1, /device:TPU:0, one launch (start us, length us, event | category | flops | bytes accessed | tf_op | source)
XLA Modules:
  0.0 517.1 jit_solution(13181663316069778548)
XLA Ops:
  8.0 2.4 stack.2
  10.4 8.1 %all-to-all-start = ((bf16[16,128,512]{2,1,0:T(8,128)(2,1)}), bf16[16,128,512]{2,1,0:T(8,128)(2,1)S(1)}, u32[]{:S(2)}, u32[]{:S(2)}) async-start(bf16[16,128,512]{2,1,0:T(8,128)(2,1)} %stack.2), calls=%async_computation | async-start | bytes 4194304 | tf_op jit(solution)/shard_map/all_to_all | solution.py:36
  18.7 29.1 %all-to-all-done = bf16[16,128,512]{2,1,0:T(8,128)(2,1)S(1)} async-done(((bf16[16,128,512]{2,1,0:T(8,128)(2,1)}), bf16[16,128,512]{2,1,0:T(8,128)(2,1)S(1)}, u32[]{:S(2)}, u32[]{:S(2)}) %all-to-all-start) | async-done | bytes 2097184 | tf_op jit(solution)/shard_map/all_to_all | solution.py:36
  47.8 4.3 convolution_convert_fusion.2
  52.0 5.6 %fusion.52 = f32[2048,1024]{1,0:T(8,128)} fusion(bf16[2048,512]{1,0:T(8,128)(2,1)S(1)} %bitcast.64, bf16[512,1024]{1,0:T(8,128)(2,1)S(1)} %copy-done.1), kind=kOutput, calls=%fused_computation.71 | convolution fusion | flops 2147483648 | bytes 11534336 | tf_op jit(solution)/shard_map/dot_general | solution.py:41
  57.6 34.8 %while.60 = (s32[]{:T(128)}, f32[8,256]{1,0:T(8,128)S(1)}, f32[8,256]{1,0:T(8,128)S(1)}, s32[8]{0:T(128)S(1)}, bf16[256,1024]{1,0:T(8,128)(2,1)}, /*index=5*/f32...) while((s32[]{:T(128)}, f32[8,256]{1,0:T(8,128)S(1)}, ...), condition=%wide.region_3.4_spmd.clone, body=%wide.region_0.3_spmd.clone.sunk | while | flops 808451584 | bytes 5326015 | solution.py:83
  58.8 2.6 fusion.85
  63.2 2.6 fusion.85
  67.5 2.6 fusion.85
  71.9 2.6 fusion.85
  76.3 2.6 fusion.85
  80.6 2.6 fusion.85
  85.0 2.6 fusion.85
  89.3 2.6 fusion.85
  92.4 28.3 %all-gather.1 = f32[64,256]{1,0:T(8,128)S(1)} all-gather(f32[8,256]{1,0:T(8,128)S(1)} %get-tuple-element.493), channel_id=3, replica_groups=mesh['ctx'=8,'head'=16] {'ctx'}, dimensions={0}, use_global_device_ids=true | all-gather | bytes 73728 | tf_op jit(solution)/shard_map/all_gather | solution.py:11
  120.7 28.2 %all-gather = f32[64,256]{1,0:T(8,128)S(1)} all-gather(f32[8,256]{1,0:T(8,128)S(1)} %get-tuple-element.492), channel_id=2, replica_groups=mesh['ctx'=8,'head'=16] {'ctx'}, dimensions={0}, use_global_device_ids=true | all-gather | bytes 73728 | tf_op jit(solution)/shard_map/all_gather | solution.py:11
  149.2 60.7 %while.61 = (s32[]{:T(128)}, f32[8,256]{1,0:T(8,128)S(1)}, s32[8]{0:T(128)S(1)}, bf16[256,1024]{1,0:T(8,128)(2,1)}, f32[2048,1024]{1,0:T(8,128)}, /*index=5*/f32...) while((s32[]{:T(128)}, f32[8,256]{1,0:T(8,128)S(1)}, ...), condition=%wide.region_8.9_spmd.clone, body=%wide.region_6.8_spmd.clone.sunk | while | flops 943193856 | bytes 5918977 | solution.py:95
  152.4 2.7 fusion.90
  160.0 2.7 fusion.90
  167.6 2.7 fusion.90
  175.2 2.7 fusion.90
  182.8 2.7 fusion.90
  190.3 2.7 fusion.90
  197.9 2.7 fusion.90
  205.5 2.7 fusion.90
  209.9 19.5 %psum.14 = f32[8,256]{1,0:T(8,128)S(1)} all-reduce(f32[8,256]{1,0:T(8,128)S(1)} %get-tuple-element.496), channel_id=1, replica_groups=mesh['ctx'=8,'head'=16] {'ctx'}, use_global_device_ids=true, to_apply=%region_9.10 | all-reduce | flops 2048 | bytes 16384 | tf_op jit(solution)/shard_map/psum | solution.py:95
  229.5 4.3 broadcast_in_dim.48
  233.8 87.8 %while.62 = (s32[]{:T(128)}, f32[256,1024]{1,0:T(8,128)S(1)}, bf16[2048,2048]{1,0:T(8,128)(2,1)}, bf16[256,1024]{1,0:T(8,128)(2,1)}, f32[2048,1024]{1,0:T(8,128)...) while((s32[]{:T(128)}, f32[256,1024]{1,0:T(8,128)S(1)}, ...), condition=%wide.region_11.12_spmd.clone, body=%wide.region_10.11_spmd.clone.sunk | while | flops 2019033088 | bytes 13522222 | solution.py:129
  233.8 2.7 fusion.102
  238.1 2.3 convolution_dynamic-update-slice_fusion.2
  244.8 2.7 fusion.102
  249.1 2.3 convolution_dynamic-update-slice_fusion.2
  255.8 2.7 fusion.102
  260.1 2.3 convolution_dynamic-update-slice_fusion.2
  266.8 2.7 fusion.102
  271.1 2.3 convolution_dynamic-update-slice_fusion.2
  277.7 2.7 fusion.102
  282.0 2.3 convolution_dynamic-update-slice_fusion.2
  288.7 2.7 fusion.102
  293.0 2.3 convolution_dynamic-update-slice_fusion.2
  299.7 2.7 fusion.102
  310.6 2.7 fusion.102
  314.9 2.3 convolution_dynamic-update-slice_fusion.2
  321.6 10.8 %fusion.45 = f32[2048,512]{1,0:T(8,128)} fusion(bf16[2048,2048]{1,0:T(8,128)(2,1)} %get-tuple-element.498, bf16[512,1024]{1,0:T(8,128)(2,1)} %param.17, bf16[512,1024]{1,0:T(8,128)(2,1)} %param.16), kind=kOutput, calls=%fused_computation.61 | convolution fusion | flops 4299161600 | bytes 14680064 | tf_op jit(solution)/shard_map/dot_general | solution.py:140
  332.5 9.8 %convolution_bitcast_fusion = f32[512,2048]{0,1:T(8,128)} fusion(bf16[2048,2048]{1,0:T(8,128)(2,1)} %get-tuple-element.498, bf16[2048,512]{1,0:T(8,128)(2,1)S(1)} %bitcast.65), kind=kOutput, calls=%fused_computation.60 | convolution fusion | flops 4294967296 | bytes 14680064 | tf_op jit(solution)/shard_map/dot_general | solution.py:133
  342.3 5.4 %copy.13 = f32[512,2048]{1,0:T(8,128)} copy(f32[512,2048]{0,1:T(8,128)} %convolution_bitcast_fusion) | data formatting | bytes 8388608
  348.3 142.2 %all-reduce.2.cloned.1.call-done = f32[2048,512]{1,0:T(8,128)} async-done(((f32[2048,512]{1,0:T(8,128)}), f32[2048,512]{1,0:T(8,128)}) %all-reduce.2.cloned.1.call-update) | async-done | bytes 4194320 | tf_op jit(solution)/shard_map/psum | solution.py:139
  494.1 15.6 %reduce-scatter.5.cloned.1.call-done = f32[32,1024]{1,0:T(8,128)} async-done(((f32[256,1024]{1,0:T(8,128)}), f32[32,1024]{1,0:T(8,128)}) %reduce-scatter.5.cloned.1.call-update) | async-done | bytes 131088 | tf_op jit(solution)/shard_map/reduce_scatter | solution.py:131
  (138 shorter events, 81.5 us)
Async XLA Ops:
  10.4 37.3 %copy-start.2 = (bf16[512,1024]{1,0:T(8,128)(2,1)S(1)}, bf16[512,1024]{1,0:T(8,128)(2,1)}, u32[]{:S(2)}) copy-start(bf16[512,1024]{1,0:T(8,128)(2,1)} %param.17) | copy-start | bytes 3145732
  10.4 37.3 %all-to-all-start = ((bf16[16,128,512]{2,1,0:T(8,128)(2,1)}), bf16[16,128,512]{2,1,0:T(8,128)(2,1)S(1)}, u32[]{:S(2)}, u32[]{:S(2)}) async-start(bf16[16,128,512]{2,1,0:T(8,128)(2,1)} %stack.2), calls=%async_computation | async-start | bytes 4194304 | tf_op jit(solution)/shard_map/all_to_all | solution.py:36
  18.6 472.0 %all-reduce.2.cloned.1.call-start = ((), (), s32[]{:S(2)}) async-start(), calls=%async_computation.4 | async-start | bytes 8388608 | tf_op jit(solution)/shard_map/psum | solution.py:139
  47.8 4.3 copy-start.1
  321.6 10.8 %copy-start = (f32[256,1024]{1,0:T(8,128)}, f32[256,1024]{1,0:T(8,128)S(1)}, u32[]{:S(2)}) copy-start(f32[256,1024]{1,0:T(8,128)S(1)} %get-tuple-element.497) | copy-start | bytes 3145732
  332.5 159.8 %reduce-scatter.7.cloned.1.call-start = ((), (), s32[]{:S(2)}) async-start(), calls=%async_computation.5 | async-start | bytes 4718592
  347.7 161.9 %reduce-scatter.5.cloned.1.call-start = ((), (), s32[]{:S(2)}) async-start(), calls=%async_computation.3 | async-start | bytes 1179648 | tf_op jit(solution)/shard_map/reduce_scatter | solution.py:131
Sparse Core Ops, SparseCore 0:
  332.6 157.9 all-reduce.1
Sparse Core Ops, SparseCore 1:
  347.8 116.6 reduce-scatter.6
  467.3 42.3 reduce-scatter.4
